TPU v7x, 32 devices: a whole 2x2x4 slice. The times are simulated.
32 devices in a mesh: row: 8 (over y, x, core), rep: 4 (over z).
Axes of the slice: x: 2, y: 2, z: 4, core: 2. Of those that a mesh axis runs over, the one named last changes fastest.
Arguments:
- features: bfloat16 [8192, 256], P('row'), may hold values from -6 to 6
- weight_self: bfloat16 [256, 256], replicated, may hold values from -0.375 to 0.375
- weight_neigh: bfloat16 [256, 256], replicated, may hold values from -0.375 to 0.375
- degrees: int32 [8192], P('row'), may hold values from 1 to 47
- tile_values: bfloat16 [8, 8, 48, 128, 128], P('row', 'rep'), may hold values from 0 to 1
- tile_blocks: int32 [8, 8, 48, 2], P('row', 'rep'), may hold values from 0 to 7
- tile_count: int32 [8, 8], P('row', 'rep'), may hold values from 1 to 48, as said below
- cotangent: bfloat16 [8192, 256], P(('row', 'rep')), may hold values from -6 to 6
Outputs:
- output: bfloat16 [8192, 256], P(('row', 'rep'))
- grad_self: float32 [256, 256], replicated
- grad_neigh: float32 [256, 256], replicated
- grad_features: bfloat16 [8192, 256], P(('row', 'rep'))
Inputs may be any that keep to these rules, and one draw needn't show every extreme that they name: `tile_count`: for some row index and section all 48 slots are live in every draw.
All inputs are finite; a program needn't handle non-finite values.
Results may differ from a plain program's by a relative error of at most 0.024.
Values may be sent and summed in bfloat16 or wider, within the bound.
A program may use at most 64 MiB of HBM per device.

v0:
```python
import functools

import jax
import jax.numpy as jnp
from jax import lax
from jax.experimental import pallas as pl
from jax.experimental.pallas import tpu as pltpu
from jax.sharding import PartitionSpec as P

MESH = pl.DeviceIdType.MESH
F32 = jnp.float32
BF16 = jnp.bfloat16
PAIR = 2


def dense_kernel(blocks_ref, count_ref, tiles_ref, out_ref, acc):
    section = pl.program_id(0)
    tile = tiles_ref.shape[-1]
    acc[...] = jnp.zeros_like(acc)

    def add(slot, carry):
        to = pl.multiple_of(blocks_ref[section, 0, slot] * tile, tile)
        src = pl.multiple_of(blocks_ref[section, 1, slot] * tile, tile)
        acc[pl.ds(to, tile), pl.ds(src, tile)] += tiles_ref[0, slot].astype(F32)
        return carry

    lax.fori_loop(0, count_ref[section], add, 0)
    out_ref[0] = acc[...].astype(BF16)


def dense_adjacency(tile_values, tile_blocks, tile_count, rows):
    sections, slots, tile, _ = tile_values.shape
    return pl.pallas_call(
        dense_kernel,
        grid=(sections,),
        out_shape=jax.ShapeDtypeStruct((sections, rows, rows), BF16),
        in_specs=[
            pl.BlockSpec(memory_space=pltpu.SMEM),
            pl.BlockSpec(memory_space=pltpu.SMEM),
            pl.BlockSpec((1, slots, tile, tile), lambda s: (s, 0, 0, 0)),
        ],
        out_specs=pl.BlockSpec((1, rows, rows), lambda s: (s, 0, 0)),
        scratch_shapes=[pltpu.VMEM((rows, rows), F32)],
        name="dense",
    )(tile_blocks, tile_count, tile_values)


def remote(src, dst, send, recv, device):
    return pltpu.make_async_remote_copy(
        src_ref=src, dst_ref=dst, send_sem=send, recv_sem=recv, device_id=device, device_id_type=MESH
    )


def layer_kernel(
    nrow, nrep, here,
    feat, wself, wneigh, deg, cot, adj_hbm,
    out, wall, gfeat,
    adj, own_feat, src, part, part_in, dagg, dagg_t, terms, pair_in, summed, plane_in, back, back_in,
    wpart, wrow_in, wrep_in, base, deg_col,
    adj_sem, loc_sem, a1s, a1r, a2s, a2r, a3s, a3r, bs, br, cs, cr, w1s, w1r, w2s, w2r, w3s, w3r,
    d0s, d0r, d1s, d1r, d2s, d2r,
):
    row, rep = lax.axis_index("row"), lax.axis_index("rep")
    rows, width = feat.shape
    lanes = src.shape[-1]
    slices = width // lanes
    share = rows // nrep
    half = nrow // PAIR
    hi, lo = row // PAIR, row % PAIR
    partner = (hi * PAIR + (1 - lo), rep)
    owner = (rep * here + row // nrep, row % nrep)
    giver = ((row % here) * nrep + rep, row // here)
    moves = jnp.logical_or(owner[0] != row, owner[1] != rep)

    adj_copy = pltpu.make_async_copy(adj_hbm, adj, adj_sem)
    adj_copy.start()

    barrier = pltpu.get_barrier_semaphore()

    def greet(device):
        pl.semaphore_signal(barrier, inc=1, device_id=device, device_id_type=MESH)

    for d in range(1, nrow):
        greet(((row + d) % nrow, rep))
    for d in range(1, nrep):
        greet((row, (rep + d) % nrep))

    @pl.when(moves)
    def _():
        greet(owner)
        greet(giver)

    for c in range(slices):
        own_feat[c] = feat[:, c * lanes : (c + 1) * lanes]

    pl.semaphore_wait(barrier, nrow - 1 + nrep - 1 + 2 * moves.astype(jnp.int32))

    is_source = row // here == rep
    first = (row - rep * here) * nrep
    own_chunk = row == rep * here + row // nrep

    def scatter(c, q):
        return remote(
            own_feat.at[c, pl.ds(q * share, share)], src.at[c, first + q],
            a1s.at[c, q], a1r.at[c], (first + q, rep),
        )

    for c in range(slices):
        for q in range(nrep):
            @pl.when(jnp.logical_and(is_source, first + q != row))
            def _():
                scatter(c, q).start()

            @pl.when(jnp.logical_and(is_source, first + q == row))
            def _():
                local = pltpu.make_async_copy(
                    own_feat.at[c, pl.ds(q * share, share)], src.at[c, row], loc_sem
                )
                local.start()
                local.wait()

    def gather(c, d):
        to = ((hi + d) % half) * PAIR + lo
        return remote(
            src.at[c, row], src.at[c, row], a2s.at[c, d - 1], a2r.at[c, d - 1], (to, rep)
        )

    def share_pair(c, d):
        chunk = ((hi + half - d) % half) * PAIR + lo
        return remote(src.at[c, chunk], src.at[c, chunk], a3s.at[c, d], a3r.at[c, d], partner)

    for c in range(slices):
        @pl.when(jnp.logical_not(own_chunk))
        def _():
            remote(src.at[c, row], src.at[c, row], a1s.at[c, 0], a1r.at[c], partner).wait_recv()

        for d in range(1, half):
            gather(c, d).start()
        share_pair(c, 0).start()

    my_feat = feat[pl.ds(pl.multiple_of(rep * share, share), share), :]
    base[...] = jnp.dot(my_feat, wself[...], preferred_element_type=F32)
    run = deg.shape[1]
    for b in range(rows // run):
        line = jnp.broadcast_to(deg[b : b + 1, :].astype(F32), (run, run))
        deg_col[pl.ds(b * run, run), :] = line.T
    adj_copy.wait()

    def partial(c, q):
        total = jnp.zeros((share, lanes), F32)
        for j in range(here):
            a = adj[j, pl.ds(pl.multiple_of(q * share, share), share), :]
            f = src[c, pl.ds(j * nrep, nrep)].reshape(rows, lanes)
            total = total + jnp.dot(a, f, preferred_element_type=F32)
        return total

    def send_part(c, d):
        to = (rep + d) % nrep
        return remote(
            part.at[c, d - 1], part_in.at[c, d - 1], bs.at[c, d - 1], br.at[c, d - 1], (row, to)
        )

    for c in range(slices):
        for d in range(1, half):
            gather(c, d).wait_recv()
            share_pair(c, d).start()
        for d in range(half):
            share_pair(c, d).wait_recv()
        for d in range(1, nrep):
            part[c, d - 1] = partial(c, (rep + d) % nrep).astype(BF16)
            send_part(c, d).start()
    degree = deg_col[pl.ds(pl.multiple_of(rep * share, share), share), :]
    aggs = []
    for c in range(slices):
        total = partial(c, rep)
        for d in range(1, nrep):
            send_part(c, d).wait_recv()
            total = total + part_in[c, d - 1].astype(F32)
        aggs.append((total / degree).astype(BF16))
    agg = jnp.concatenate(aggs, axis=1)

    pre = base[...] + jnp.dot(agg, wneigh[...], preferred_element_type=F32)
    sig = jax.nn.sigmoid(pre)
    gpre = (cot[...].astype(F32) * sig * (1.0 + pre * (1.0 - sig))).astype(BF16)

    def send_dagg(c, d):
        return remote(
            dagg.at[c, rep], dagg.at[c, rep], cs.at[c, d - 1], cr.at[c, d - 1],
            (row, (rep + d) % nrep),
        )

    for c in range(slices):
        back_t = lax.dot_general(
            gpre, wneigh[c * lanes : (c + 1) * lanes, :], (((1,), (1,)), ((), ())),
            preferred_element_type=F32,
        )
        dagg[c, rep] = (back_t / degree).astype(BF16)
        for d in range(1, nrep):
            send_dagg(c, d).start()
    ws = lax.dot_general(my_feat, gpre, (((0,), (0,)), ((), ())), preferred_element_type=F32)
    wn = lax.dot_general(agg, gpre, (((0,), (0,)), ((), ())), preferred_element_type=F32)
    piece = wpart.shape[1]
    wpart[pl.ds(0, half)] = ws.astype(BF16).reshape(half, piece, width)
    wpart[pl.ds(half, half)] = wn.astype(BF16).reshape(half, piece, width)

    def send_w1(d):
        to = (row + d) % nrow
        return remote(wpart.at[to], wrow_in.at[d - 1], w1s.at[d - 1], w1r.at[d - 1], (to, rep))

    for d in range(1, nrow):
        send_w1(d).start()
    out[...] = (pre * sig).astype(BF16)
    base[...] = lax.dot_general(gpre, wself[...], (((1,), (1,)), ((), ())), preferred_element_type=F32)

    unit = max(share, 128)
    per_unit = unit // share

    def send_pair(c, h):
        return remote(
            terms.at[c, h * PAIR + (1 - lo)], pair_in.at[c, h], d0s.at[c, h], d0r.at[c, h], partner
        )

    def send_plane(c, d):
        h = (hi + d) % half
        return remote(
            summed.at[c, h], plane_in.at[c, d - 1], d1s.at[c, d - 1], d1r.at[c, d - 1],
            (h * PAIR + lo, rep),
        )

    def to_owner(c):
        return remote(back.at[c], back_in.at[c], d2s.at[c], d2r.at[c], owner)

    def make_terms(c):
        for d in range(1, nrep):
            remote(
                dagg.at[c, rep], dagg.at[c, (rep + nrep - d) % nrep], cs.at[c, d - 1], cr.at[c, d - 1],
                (row, rep),
            ).wait_recv()
        dagg_t[...] = dagg[c].reshape(rows, lanes).T
        for u in range(here * rows // unit):
            j, col = divmod(u * unit, rows)
            t = jnp.dot(dagg_t[...], adj[j, :, col : col + unit], preferred_element_type=F32)
            terms[c, pl.ds(u * per_unit, per_unit)] = t.T.astype(BF16).reshape(per_unit, share, lanes)
            for r in range(u * per_unit, (u + 1) * per_unit):
                @pl.when(r % PAIR != lo)
                def _():
                    send_pair(c, r // PAIR).start()

    def add_pair(c):
        for d in list(range(1, half)) + [0]:
            h = (hi + d) % half
            send_pair(c, h).wait_recv()
            both = terms[c, h * PAIR + lo].astype(F32) + pair_in[c, h].astype(F32)
            if d > 0:
                summed[c, h] = both.astype(BF16)
                send_plane(c, d).start()
            else:
                back_sum[c] = both

    def add_plane(c):
        both = back_sum[c]
        for d in range(1, half):
            send_plane(c, d).wait_recv()
            both = both + plane_in[c, d - 1].astype(F32)
        back[c] = both.astype(BF16)

        @pl.when(moves)
        def _():
            to_owner(c).start()

    back_sum = {}
    for c in range(slices):
        make_terms(c)
        if c + 1 < slices:
            add_pair(c)

    wsum = wpart[row].astype(F32)
    for d in range(1, nrow):
        send_w1(d).wait_recv()
        wsum = wsum + wrow_in[d - 1].astype(F32)
    wrep_in[rep] = wsum.astype(BF16)

    def send_w2(d):
        return remote(
            wrep_in.at[rep], wrep_in.at[rep], w2s.at[d - 1], w2r.at[d - 1], (row, (rep + d) % nrep)
        )

    for d in range(1, nrep):
        send_w2(d).start()
    add_pair(slices - 1)
    for c in range(slices - 1):
        add_plane(c)

    for d in range(1, nrep):
        remote(
            wrep_in.at[rep], wrep_in.at[(rep + nrep - d) % nrep], w2s.at[d - 1], w2r.at[d - 1], (row, rep)
        ).wait_recv()
    wsum = wrep_in[0].astype(F32)
    for k in range(1, nrep):
        wsum = wsum + wrep_in[k].astype(F32)
    wall[row] = wsum.astype(BF16)

    def send_w3(d):
        return remote(
            wall.at[row], wall.at[row], w3s.at[d - 1], w3r.at[d - 1], ((row + d) % nrow, rep)
        )

    for d in range(1, nrow):
        send_w3(d).start()
    add_plane(slices - 1)
    for d in range(1, nrow):
        remote(
            wall.at[row], wall.at[(row + nrow - d) % nrow], w3s.at[d - 1], w3r.at[d - 1], (row, rep)
        ).wait_recv()

    for c in range(slices):
        cols = slice(c * lanes, (c + 1) * lanes)

        @pl.when(moves)
        def _():
            to_owner(c).wait_recv()
            gfeat[:, cols] = (base[:, cols] + back_in[c].astype(F32)).astype(BF16)

        @pl.when(jnp.logical_not(moves))
        def _():
            gfeat[:, cols] = (base[:, cols] + back[c].astype(F32)).astype(BF16)

    for c in range(slices):
        for q in range(nrep):
            @pl.when(jnp.logical_and(is_source, first + q != row))
            def _():
                scatter(c, q).wait_send()

        for d in range(1, half):
            gather(c, d).wait_send()
            send_plane(c, d).wait_send()
        for d in range(half):
            share_pair(c, d).wait_send()
            send_pair(c, d).wait_send()
        for d in range(1, nrep):
            send_part(c, d).wait_send()
            send_dagg(c, d).wait_send()

        @pl.when(moves)
        def _():
            to_owner(c).wait_send()

    for d in range(1, nrep):
        send_w2(d).wait_send()
    for d in range(1, nrow):
        send_w1(d).wait_send()
        send_w3(d).wait_send()


def close_kernel(out_in, wall, gfeat_in, out, gself, gneigh, gfeat):
    half = wall.shape[0] // 2
    out[...] = out_in[...]
    gfeat[...] = gfeat_in[...]
    gself[...] = wall[pl.ds(0, half)].reshape(gself.shape).astype(F32)
    gneigh[...] = wall[pl.ds(half, half)].reshape(gneigh.shape).astype(F32)


def body(
    nrow, nrep,
    features, weight_self, weight_neigh, degrees, tile_values, tile_blocks, tile_count, cotangent,
):
    rows, width = features.shape
    here = tile_values.shape[1]
    tile = tile_values.shape[-1]
    share = rows // nrep
    half = nrow // PAIR
    piece = 2 * width // nrow
    lanes = 128
    slices = width // lanes
    adjacency = dense_adjacency(
        tile_values[0], tile_blocks.transpose(0, 1, 3, 2)[0], tile_count[0], rows
    )
    sems = pltpu.SemaphoreType.DMA
    vmem = pl.BlockSpec(memory_space=pltpu.VMEM)

    def buf(*shape):
        return pltpu.VMEM(shape, BF16)

    out, wall, gfeat = pl.pallas_call(
        functools.partial(layer_kernel, nrow, nrep, here),
        out_shape=(
            jax.ShapeDtypeStruct((share, width), BF16),
            jax.ShapeDtypeStruct((nrow, piece, width), BF16),
            jax.ShapeDtypeStruct((share, width), BF16),
        ),
        in_specs=[vmem] * 5 + [pl.BlockSpec(memory_space=pl.ANY)],
        out_specs=(vmem,) * 3,
        scratch_shapes=[
            buf(here, rows, rows),
            buf(slices, rows, lanes),
            buf(slices, nrow, share, lanes),
            buf(slices, nrep - 1, share, lanes),
            buf(slices, nrep - 1, share, lanes),
            buf(slices, nrep, share, lanes),
            buf(lanes, rows),
            buf(slices, nrow, share, lanes),
            buf(slices, half, share, lanes),
            buf(slices, half, share, lanes),
            buf(slices, half - 1, share, lanes),
            buf(slices, share, lanes),
            buf(slices, share, lanes),
            buf(nrow, piece, width),
            buf(nrow - 1, piece, width),
            buf(nrep, piece, width),
            pltpu.VMEM((share, width), F32),
            pltpu.VMEM((rows, tile), F32),
            sems, sems,
            sems((slices, nrep)), sems((slices,)),
            sems((slices, half - 1)), sems((slices, half - 1)),
            sems((slices, half)), sems((slices, half)),
            sems((slices, nrep - 1)), sems((slices, nrep - 1)),
            sems((slices, nrep - 1)), sems((slices, nrep - 1)),
            sems((nrow - 1,)), sems((nrow - 1,)),
            sems((nrep - 1,)), sems((nrep - 1,)),
            sems((nrow - 1,)), sems((nrow - 1,)),
            sems((slices, half)), sems((slices, half)),
            sems((slices, half - 1)), sems((slices, half - 1)),
            sems((slices,)), sems((slices,)),
        ],
        compiler_params=pltpu.CompilerParams(collective_id=0, has_side_effects=True),
        name="layer",
    )(features, weight_self, weight_neigh, degrees.reshape(rows // tile, tile), cotangent, adjacency)
    out, grad_self, grad_neigh, gfeat = pl.pallas_call(
        close_kernel,
        out_shape=(
            jax.ShapeDtypeStruct((share, width), BF16),
            jax.ShapeDtypeStruct((width, width), F32),
            jax.ShapeDtypeStruct((width, width), F32),
            jax.ShapeDtypeStruct((share, width), BF16),
        ),
        in_specs=[vmem] * 3,
        out_specs=(vmem,) * 4,
        name="close",
    )(out, wall, gfeat)
    return out, grad_self, grad_neigh, gfeat


def solution(mesh):
    in_specs = (
        P("row", None),
        P(),
        P(),
        P("row"),
        P("row", "rep", None, None, None),
        P("row", "rep", None, None),
        P("row", "rep"),
        P(("row", "rep"), None),
    )
    out_specs = (P(("row", "rep"), None), P(), P(), P(("row", "rep"), None))
    run = functools.partial(body, mesh.shape["row"], mesh.shape["rep"])
    return jax.shard_map(run, mesh=mesh, in_specs=in_specs, out_specs=out_specs, check_vma=False)
```

profile of v0, /device:TPU:7, one launch (start us, length us, event | category | flops | bytes accessed | tf_op | source)
XLA Modules:
  0.0 65.6 jit_solution(15050188754709693131)
XLA Ops:
  0.6 4.0 %dense.1.adj_hbm = bf16[2,1024,1024]{2,1,0:T(8,128)(2,1)} custom-call(s32[2,2,48]{2,1,0:T(2,128)} %bitcast.8, s32[2]{0:T(128)} %bitcast.9, bf16[2,48,128,128]{3,2,1,0:T(8,128)(2,1)} %bitcast.6), custom_call_target="tpu_custom_call" | custom-call | tf_op jit(solution)/shard_map/dense/pallas_call | solution.py:33
  4.6 59.1 %layer.1 = (bf16[256,256]{1,0:T(8,128)(2,1)}, bf16[8,64,256]{2,1,0:T(8,128)(2,1)}, bf16[256,256]{1,0:T(8,128)(2,1)}) custom-call(bf16[1024,256]{1,0:T(8,128)(2,1)} %feat.1, bf16[256,256]{1,0:T(8,128)(2,1)} %wself.1, bf16[256,256]{1,0:T(8,128)(2,1)} %wneigh.1, s32[8,128]{1,0:T(8,128)} %bitcast.7, bf16[256,256]{1,0:T(8,128)(2,1)} %cot.1, ...), custom_call_target="tpu_custom_call" | custom-call | tf_op jit(solution)/shard_map/layer/pallas_call | solution.py:384
  63.7 1.9 %close.1 = (bf16[256,256]{1,0:T(8,128)(2,1)}, f32[256,256]{1,0:T(8,128)}, f32[256,256]{1,0:T(8,128)}, bf16[256,256]{1,0:T(8,128)(2,1)}) custom-call(bf16[256,256]{1,0:T(8,128)(2,1)} %get-tuple-element.7.out_in, bf16[8,64,256]{2,1,0:T(8,128)(2,1)} %get-tuple-element.8.wall, bf16[256,256]{1,0:T(8,128)(2,1)} %get-tuple-element.9.gfeat_in), custom_call_target="tpu_custom_call" | custom-call | tf_op jit(solution)/shard_map/close/pallas_call | solution.py:428
where the time goes:
time: 65.8 us; the launch traced here: 65.6 us
  Pallas kernels  65 us (99%)
    pallas_call x1, Pallas kernels, body(): pl.pallas_call(functools.partial(layer_kernel, nrow, nrep, here), out_sha...  59.1 us
    pallas_call x1, Pallas kernels, dense_adjacency(): pl.pallas_call(dense_kernel, grid=(sections,), out_shape=jax.ShapeDtypeSt...  3.96 us
    pallas_call x1, Pallas kernels, body(): pl.pallas_call(close_kernel, out_shape=(jax.ShapeDtypeStruct((share, widt...  1.95 us

commit v1 on v0

v1 whole, which is shorter than its diff:
```python
import functools

import jax
import jax.numpy as jnp
from jax import lax
from jax.experimental import pallas as pl
from jax.experimental.pallas import tpu as pltpu
from jax.sharding import PartitionSpec as P

MESH = pl.DeviceIdType.MESH
F32 = jnp.float32
BF16 = jnp.bfloat16
PAIR = 2
PARTS = 4


def remote(src, dst, send, recv, device):
    return pltpu.make_async_remote_copy(
        src_ref=src, dst_ref=dst, send_sem=send, recv_sem=recv, device_id=device, device_id_type=MESH
    )


def bits_of(n):
    return (n - 1).bit_length()


def xor(a, b, n):
    total = 0
    for k in range(bits_of(n)):
        w = 2**k
        total = total + ((a // w + b // w) % 2) * w
    return total


def mirror(a, n):
    total = 0
    top = bits_of(n)
    for k in range(top):
        total = total + ((a // 2**k) % 2) * 2 ** (top - 1 - k)
    return total


def layer_kernel(
    nrow, nrep, here,
    feat_hbm, wself, wneigh, deg, cot, tiles_hbm, blocks, count,
    out, wall, gfeat,
    tiles, runs, adj, keys, tab_v, tab_s, my_feat, src, mine, part, part_in, agg_all, gpre_all,
    dagg, dagg_t, terms, pair_in, summed, plane_in, back, back_in,
    wpart, wrow_in, wrep_in, base, deg_col,
    tile_sem, tab_sem, feat_sem, own_sem,
    p1s, p1r, p1ps, p1pr, bs, br, es, er, cs, cr, fs, fr, w1s, w1r, w2s, w2r, w3s, w3r,
    d0s, d0r, d1s, d1r, d2s, d2r,
):
    row, rep = lax.axis_index("row"), lax.axis_index("rep")
    rows, width = feat_hbm.shape
    lanes = src.shape[-1]
    slices = width // lanes
    share = rows // nrep
    half = nrow // PAIR
    tile = tiles.shape[-1]
    slots = tiles.shape[1]
    nblk = rows // tile
    hi, lo = row // PAIR, row % PAIR
    hx, hy = hi % PAIR, hi // PAIR
    ny = half // PAIR
    sx, sy = rep % PAIR, rep // PAIR
    is_src = hi == rep
    is_x = jnp.logical_and(hy == sy, hx != sx)
    is_y = jnp.logical_and(hx == sx, hy != sy)
    is_d = jnp.logical_and(hx != sx, hy != sy)
    partner = (hi * PAIR + (1 - lo), rep)
    my_q = xor(hi, mirror(rep, nrep), nrep)
    owner = (rep * PAIR + lo, my_q)
    giver = (xor(rep, mirror(hi, nrep), nrep) * PAIR + lo, hi)
    moves = jnp.logical_or(owner[0] != row, owner[1] != rep)

    barrier = pltpu.get_barrier_semaphore()

    def greet(device):
        pl.semaphore_signal(barrier, inc=1, device_id=device, device_id_type=MESH)

    for d in range(1, nrow):
        greet(((row + d) % nrow, rep))
    for d in range(1, nrep):
        greet((row, (rep + d) % nrep))

    @pl.when(moves)
    def _():
        greet(owner)
        greet(giver)

    def own_copy(c, k):
        return pltpu.make_async_copy(
            feat_hbm.at[pl.ds(k * share, share), pl.ds(c * lanes, lanes)],
            src.at[c, lo * nrep + k], own_sem.at[c, k],
        )

    @pl.when(is_src)
    def _():
        for c in range(slices):
            for k in range(nrep):
                own_copy(c, k).start()

    tile_copies = [
        pltpu.make_async_copy(tiles_hbm.at[j], tiles.at[j], tile_sem.at[j]) for j in range(here)
    ]
    for copy in tile_copies:
        copy.start()
    feat_copy = pltpu.make_async_copy(
        feat_hbm.at[pl.ds(pl.multiple_of(rep * share, share), share)], my_feat, feat_sem
    )
    feat_copy.start()

    side = keys.shape[-1]
    at_row = lax.broadcasted_iota(jnp.int32, (side, side), 0)
    at_col = lax.broadcasted_iota(jnp.int32, (side, side), 1)
    for j in range(here):
        keys[...] = jnp.full(keys.shape, -1, jnp.int32)
        keys[0:1, 0:slots] = blocks[j, 0:1, :] * nblk + blocks[j, 1:2, :]
        line = jnp.broadcast_to(keys[0:1, :], (side, side))
        column = line.T
        before = jnp.where(jnp.logical_and(column == line, at_row < at_col), at_row + 1, 0)
        latest = jnp.where(jnp.logical_and(column == at_col, at_row < count[j]), at_row + 1, 0)
        tab_v[2 * j : 2 * j + 1, :] = jnp.max(before, axis=0, keepdims=True)
        tab_v[2 * j + 1 : 2 * j + 2, :] = jnp.max(latest, axis=0, keepdims=True)
    tab_copy = pltpu.make_async_copy(tab_v, tab_s, tab_sem)
    tab_copy.start()
    run = deg.shape[1]
    for b in range(rows // run):
        line = jnp.broadcast_to(deg[b : b + 1, :].astype(F32), (run, run))
        deg_col[pl.ds(b * run, run), :] = line.T
    tab_copy.wait()

    pl.semaphore_wait(barrier, nrow - 1 + nrep - 1 + 2 * moves.astype(jnp.int32))

    def hop(c, k, i, h):
        at = src.at[c, lo * nrep + k]
        return remote(at, at, p1s.at[c, k, i], p1r.at[c, k], (h * PAIR + lo, rep))

    def x_peer():
        return hy * PAIR + (1 - hx)

    def y_peer(d):
        return ((hy + d) % ny) * PAIR + hx

    def to_partner(c, k):
        at = src.at[c, lo * nrep + k]
        return remote(at, at, p1ps.at[c, k], p1pr.at[c, k], partner)

    def from_partner(c, k):
        at = src.at[c, (1 - lo) * nrep + k]
        return remote(at, at, p1ps.at[c, k], p1pr.at[c, k], partner)

    first, second = list(range(nrep // 2)), list(range(nrep // 2, nrep))

    @pl.when(is_src)
    def _():
        for c in range(slices):
            for k in range(nrep):
                own_copy(c, k).wait()
            for kx, ky in zip(first + second, second + first):
                hop(c, kx, 0, x_peer()).start()
                for d in range(1, ny):
                    hop(c, ky, d, y_peer(d)).start()
            for k in range(nrep):
                to_partner(c, k).start()

    for j in range(here):
        tile_copies[j].wait()
        runs[0] = jnp.zeros((tile, tile), F32)

        def add(slot, carry):
            runs[slot + 1] = tiles[j, slot].astype(F32) + runs[tab_s[2 * j, slot]]
            return carry

        lax.fori_loop(0, slots, add, 0)

        def place(b, carry):
            for c in range(nblk):
                block = runs[tab_s[2 * j + 1, b * nblk + c]]
                adj[j, pl.ds(pl.multiple_of(b * tile, tile), tile), c * tile : (c + 1) * tile] = block.astype(BF16)
            return carry

        lax.fori_loop(0, nblk, place, 0)

    def relay(c):
        @pl.when(is_x)
        def _():
            for k in first + second:
                hop(c, k, 0, hi).wait_recv()
                if k in first:
                    for d in range(1, ny):
                        hop(c, k, d, y_peer(d)).start()
                to_partner(c, k).start()

        @pl.when(is_y)
        def _():
            for k in second + first:
                hop(c, k, 0, hi).wait_recv()
                if k in second:
                    hop(c, k, 0, x_peer()).start()
                to_partner(c, k).start()

        @pl.when(is_d)
        def _():
            for pair in zip(first, second):
                for k in pair:
                    hop(c, k, 0, hi).wait_recv()
                    to_partner(c, k).start()

        for k in range(nrep):
            from_partner(c, k).wait_recv()

    def partial(c, q):
        total = jnp.zeros((share, lanes), F32)
        for j in range(here):
            a = adj[j, pl.ds(pl.multiple_of(q * share, share), share), :]
            f = src[c, pl.ds(j * nrep, nrep)].reshape(rows, lanes)
            total = total + jnp.dot(a, f, preferred_element_type=F32)
        return total

    last = slices - 1
    step = share // PARTS

    def send_part(c, d):
        to = (rep + d) % nrep
        return remote(
            part.at[c, d - 1], part_in.at[c, d - 1], bs.at[c, d - 1], br.at[c, d - 1], (row, to)
        )

    def send_step(d, i):
        to = (rep + d) % nrep
        at = (last, d - 1, pl.ds(i * step, step))
        return remote(part.at[at], part_in.at[at], es.at[d - 1, i], er.at[d - 1, i], (row, to))

    for c in range(slices):
        relay(c)
        for d in range(1, nrep):
            part[c, d - 1] = partial(c, (rep + d) % nrep).astype(BF16)
            if c < last:
                send_part(c, d).start()
        if c == last:
            for i in range(PARTS):
                for d in range(1, nrep):
                    send_step(d, i).start()
        mine[c] = partial(c, rep)
    feat_copy.wait()
    base[...] = jnp.dot(my_feat[...], wself[...], preferred_element_type=F32)

    def send_dagg(c, d, i):
        at = (c, rep, pl.ds(i * step, step))
        return remote(
            dagg.at[at], dagg.at[at], cs.at[c, d - 1, i], cr.at[c, d - 1, i], (row, (rep + d) % nrep)
        )

    for c in range(last):
        for d in range(1, nrep):
            send_part(c, d).wait_recv()
            mine[c] = mine[c] + part_in[c, d - 1].astype(F32)
    for i in range(PARTS):
        at = pl.ds(i * step, step)
        degree = deg_col[pl.ds(pl.multiple_of(rep * share + i * step, step), step), :]
        total = mine[last, at]
        for d in range(1, nrep):
            send_step(d, i).wait_recv()
            total = total + part_in[last, d - 1, at].astype(F32)
        sums = [mine[c, at] for c in range(last)] + [total]
        agg = jnp.concatenate([(s / degree).astype(BF16) for s in sums], axis=1)
        agg_all[at] = agg
        pre = base[at] + jnp.dot(agg, wneigh[...], preferred_element_type=F32)
        sig = jax.nn.sigmoid(pre)
        gpre = (cot[at].astype(F32) * sig * (1.0 + pre * (1.0 - sig))).astype(BF16)
        gpre_all[at] = gpre
        back_t = lax.dot_general(gpre, wneigh[...], (((1,), (1,)), ((), ())), preferred_element_type=F32)
        for c in range(slices):
            dagg[c, rep, at] = (back_t[:, c * lanes : (c + 1) * lanes] / degree).astype(BF16)
        for d in range(1, nrep):
            send_dagg(0, d, i).start()
        out[at] = (pre * sig).astype(BF16)
    for c in range(1, slices):
        for i in range(PARTS):
            for d in range(1, nrep):
                send_dagg(c, d, i).start()

    gpre = gpre_all[...]
    ws = lax.dot_general(my_feat[...], gpre, (((0,), (0,)), ((), ())), preferred_element_type=F32)
    wn = lax.dot_general(agg_all[...], gpre, (((0,), (0,)), ((), ())), preferred_element_type=F32)
    piece = wpart.shape[1]
    wpart[pl.ds(0, half)] = ws.astype(BF16).reshape(half, piece, width)
    wpart[pl.ds(half, half)] = wn.astype(BF16).reshape(half, piece, width)

    def send_w1(d):
        to = (row + d) % nrow
        return remote(wpart.at[to], wrow_in.at[d - 1], w1s.at[d - 1], w1r.at[d - 1], (to, rep))

    for d in range(1, nrow):
        send_w1(d).start()
    base[...] = lax.dot_general(gpre, wself[...], (((1,), (1,)), ((), ())), preferred_element_type=F32)

    unit = max(share, 128)
    per_unit = unit // share

    def send_pair(c, q):
        return remote(
            terms.at[c, (1 - lo) * nrep + q], pair_in.at[c, q], d0s.at[c, q], d0r.at[c, q], partner
        )

    def send_plane(c, e):
        return remote(
            summed.at[c, e - 1], plane_in.at[c, e - 1], d1s.at[c, e - 1], d1r.at[c, e - 1],
            (xor(hi, e, half) * PAIR + lo, rep),
        )

    def to_owner(c):
        return remote(back.at[c], back_in.at[c], d2s.at[c], d2r.at[c], owner)

    def make_terms(c):
        for i in range(PARTS):
            for d in range(1, nrep):
                at = (c, (rep + nrep - d) % nrep, pl.ds(i * step, step))
                remote(
                    dagg.at[at], dagg.at[at], cs.at[c, d - 1, i], cr.at[c, d - 1, i], (row, rep)
                ).wait_recv()
        dagg_t[...] = dagg[c].reshape(rows, lanes).T
        for j in (1 - lo, lo):
            for u in range(rows // unit):
                t = jnp.dot(
                    dagg_t[...], adj[j, :, u * unit : (u + 1) * unit], preferred_element_type=F32
                ).astype(BF16)
                for v in range(per_unit):
                    q = u * per_unit + v
                    terms[c, j * nrep + q] = t[:, v * share : (v + 1) * share]
                    if j is not lo:
                        send_pair(c, q).start()

    def add_pair(c):
        for e in list(range(half - 1, 0, -1)) + [0]:
            q = xor(xor(hi, e, half), mirror(rep, nrep), nrep)
            send_pair(c, q).wait_recv()
            both = terms[c, lo * nrep + q].astype(F32) + pair_in[c, q].astype(F32)
            if e > 0:
                summed[c, e - 1] = both.astype(BF16)
                send_plane(c, e).start()
            else:
                back_sum[c] = both

    def add_plane(c):
        both = back_sum[c]
        for e in range(1, half):
            send_plane(c, e).wait_recv()
            both = both + plane_in[c, e - 1].astype(F32)
        back[c] = both.astype(BF16)

        @pl.when(moves)
        def _():
            to_owner(c).start()

    back_sum = {}
    for c in range(slices):
        make_terms(c)
        if c + 1 < slices:
            add_pair(c)

    wsum = wpart[row].astype(F32)
    for d in range(1, nrow):
        send_w1(d).wait_recv()
        wsum = wsum + wrow_in[d - 1].astype(F32)
    wrep_in[rep] = wsum.astype(BF16)

    def send_w2(d):
        return remote(
            wrep_in.at[rep], wrep_in.at[rep], w2s.at[d - 1], w2r.at[d - 1], (row, (rep + d) % nrep)
        )

    for d in range(1, nrep):
        send_w2(d).start()
    add_pair(slices - 1)
    for c in range(slices - 1):
        add_plane(c)

    for d in range(1, nrep):
        remote(
            wrep_in.at[rep], wrep_in.at[(rep + nrep - d) % nrep], w2s.at[d - 1], w2r.at[d - 1], (row, rep)
        ).wait_recv()
    wsum = wrep_in[0].astype(F32)
    for k in range(1, nrep):
        wsum = wsum + wrep_in[k].astype(F32)
    wall[row] = wsum.astype(BF16)

    def send_w3(d):
        return remote(
            wall.at[row], wall.at[row], w3s.at[d - 1], w3r.at[d - 1], ((row + d) % nrow, rep)
        )

    for d in range(1, nrow):
        send_w3(d).start()
    add_plane(slices - 1)
    for d in range(1, nrow):
        remote(
            wall.at[row], wall.at[(row + nrow - d) % nrow], w3s.at[d - 1], w3r.at[d - 1], (row, rep)
        ).wait_recv()

    for c in range(slices):
        cols = slice(c * lanes, (c + 1) * lanes)

        @pl.when(moves)
        def _():
            to_owner(c).wait_recv()
            gfeat[:, cols] = (base[:, cols] + back_in[c].astype(F32).T).astype(BF16)

        @pl.when(jnp.logical_not(moves))
        def _():
            gfeat[:, cols] = (base[:, cols] + back[c].astype(F32).T).astype(BF16)

    for c in range(slices):
        @pl.when(is_src)
        def _():
            for k in range(nrep):
                hop(c, k, 0, x_peer()).wait_send()
                for d in range(1, ny):
                    hop(c, k, d, y_peer(d)).wait_send()

        @pl.when(is_x)
        def _():
            for k in first:
                for d in range(1, ny):
                    hop(c, k, d, y_peer(d)).wait_send()

        @pl.when(is_y)
        def _():
            for k in second:
                hop(c, k, 0, x_peer()).wait_send()

        for k in range(nrep):
            to_partner(c, k).wait_send()
            send_pair(c, k).wait_send()
        for d in range(1, nrep):
            if c < last:
                send_part(c, d).wait_send()
            for i in range(PARTS):
                if c == last:
                    send_step(d, i).wait_send()
                send_dagg(c, d, i).wait_send()
        for e in range(1, half):
            send_plane(c, e).wait_send()

        @pl.when(moves)
        def _():
            to_owner(c).wait_send()

    for d in range(1, nrep):
        send_w2(d).wait_send()
    for d in range(1, nrow):
        send_w1(d).wait_send()
        send_w3(d).wait_send()


def close_kernel(out_in, wall, gfeat_in, out, gself, gneigh, gfeat):
    half = wall.shape[0] // 2
    out[...] = out_in[...]
    gfeat[...] = gfeat_in[...]
    gself[...] = wall[pl.ds(0, half)].reshape(gself.shape).astype(F32)
    gneigh[...] = wall[pl.ds(half, half)].reshape(gneigh.shape).astype(F32)


def body(
    nrow, nrep,
    features, weight_self, weight_neigh, degrees, tile_values, tile_blocks, tile_count, cotangent,
):
    rows, width = features.shape
    here, slots, tile = tile_values.shape[1], tile_values.shape[2], tile_values.shape[-1]
    share = rows // nrep
    half = nrow // PAIR
    ny = half // PAIR
    piece = 2 * width // nrow
    lanes = 128
    slices = width // lanes
    assert here == PAIR and half == nrep and (rows // tile) ** 2 <= 128 and slots <= 128
    sems = pltpu.SemaphoreType.DMA
    vmem = pl.BlockSpec(memory_space=pltpu.VMEM)
    anywhere = pl.BlockSpec(memory_space=pl.ANY)

    def buf(*shape):
        return pltpu.VMEM(shape, BF16)

    out, wall, gfeat = pl.pallas_call(
        functools.partial(layer_kernel, nrow, nrep, here),
        out_shape=(
            jax.ShapeDtypeStruct((share, width), BF16),
            jax.ShapeDtypeStruct((nrow, piece, width), BF16),
            jax.ShapeDtypeStruct((share, width), BF16),
        ),
        in_specs=[anywhere] + [vmem] * 4 + [anywhere, vmem, pl.BlockSpec(memory_space=pltpu.SMEM)],
        out_specs=(vmem,) * 3,
        scratch_shapes=[
            buf(here, slots, tile, tile),
            pltpu.VMEM((slots + 1, tile, tile), F32),
            buf(here, rows, rows),
            pltpu.VMEM((8, 128), jnp.int32),
            pltpu.VMEM((8, 128), jnp.int32),
            pltpu.SMEM((8, 128), jnp.int32),
            buf(share, width),
            buf(slices, nrow, share, lanes),
            pltpu.VMEM((slices, share, lanes), F32),
            buf(slices, nrep - 1, share, lanes),
            buf(slices, nrep - 1, share, lanes),
            buf(share, width),
            buf(share, width),
            buf(slices, nrep, share, lanes),
            buf(lanes, rows),
            buf(slices, nrow, lanes, share),
            buf(slices, nrep, lanes, share),
            buf(slices, half - 1, lanes, share),
            buf(slices, half - 1, lanes, share),
            buf(slices, lanes, share),
            buf(slices, lanes, share),
            buf(nrow, piece, width),
            buf(nrow - 1, piece, width),
            buf(nrep, piece, width),
            pltpu.VMEM((share, width), F32),
            pltpu.VMEM((rows, tile), F32),
            sems((here,)), sems, sems, sems((slices, nrep)),
            sems((slices, nrep, ny)), sems((slices, nrep)), sems((slices, nrep)), sems((slices, nrep)),
            sems((slices, nrep - 1)), sems((slices, nrep - 1)),
            sems((nrep - 1, PARTS)), sems((nrep - 1, PARTS)),
            sems((slices, nrep - 1, PARTS)), sems((slices, nrep - 1, PARTS)),
            sems, sems,
            sems((nrow - 1,)), sems((nrow - 1,)),
            sems((nrep - 1,)), sems((nrep - 1,)),
            sems((nrow - 1,)), sems((nrow - 1,)),
            sems((slices, nrep)), sems((slices, nrep)),
            sems((slices, half - 1)), sems((slices, half - 1)),
            sems((slices,)), sems((slices,)),
        ],
        compiler_params=pltpu.CompilerParams(collective_id=0, has_side_effects=True),
        name="layer",
    )(
        features, weight_self, weight_neigh, degrees.reshape(rows // tile, tile), cotangent,
        tile_values[0], tile_blocks.transpose(0, 1, 3, 2)[0], tile_count[0],
    )
    out, grad_self, grad_neigh, gfeat = pl.pallas_call(
        close_kernel,
        out_shape=(
            jax.ShapeDtypeStruct((share, width), BF16),
            jax.ShapeDtypeStruct((width, width), F32),
            jax.ShapeDtypeStruct((width, width), F32),
            jax.ShapeDtypeStruct((share, width), BF16),
        ),
        in_specs=[vmem] * 3,
        out_specs=(vmem,) * 4,
        name="close",
    )(out, wall, gfeat)
    return out, grad_self, grad_neigh, gfeat


def solution(mesh):
    in_specs = (
        P("row", None),
        P(),
        P(),
        P("row"),
        P("row", "rep", None, None, None),
        P("row", "rep", None, None),
        P("row", "rep"),
        P(("row", "rep"), None),
    )
    out_specs = (P(("row", "rep"), None), P(), P(), P(("row", "rep"), None))
    run = functools.partial(body, mesh.shape["row"], mesh.shape["rep"])
    return jax.shard_map(run, mesh=mesh, in_specs=in_specs, out_specs=out_specs, check_vma=False)
```

time: 65.8 us -> 58.7 us (0.89)
  the two profiles are of different devices: /device:TPU:7 before, /device:TPU:0 now
where the time goes in v1:
time: 58.7 us; the launch traced here: 58.6 us
  Pallas kernels  57.9 us (99%)
  between operations  0.64 us (1%)
    pallas_call x1, Pallas kernels, body(): pl.pallas_call(functools.partial(layer_kernel, nrow, nrep, here), out_sha...  56 us
    pallas_call x1, Pallas kernels, body(): pl.pallas_call(close_kernel, out_shape=(jax.ShapeDtypeStruct((share, widt...  1.95 us

profile of v1, /device:TPU:0, one launch (start us, length us, event | category | flops | bytes accessed | tf_op | source)
XLA Modules:
  0.0 58.6 jit_solution(712840551267899723)
XLA Ops:
  0.6 56.0 %layer.1 = (bf16[256,256]{1,0:T(8,128)(2,1)}, bf16[8,64,256]{2,1,0:T(8,128)(2,1)}, bf16[256,256]{1,0:T(8,128)(2,1)}) custom-call(bf16[1024,256]{1,0:T(8,128)(2,1)} %feat_hbm.1, bf16[256,256]{1,0:T(8,128)(2,1)} %wself.1, bf16[256,256]{1,0:T(8,128)(2,1)} %wneigh.1, s32[8,128]{1,0:T(8,128)} %bitcast.7, bf16[256,256]{1,0:T(8,128)(2,1)} %cot.1, ...), custom_call_target="tpu_custom_call" | custom-call | tf_op jit(solution)/shard_map/layer/pallas_call | solution.py:486
  56.6 1.9 %close.1 = (bf16[256,256]{1,0:T(8,128)(2,1)}, f32[256,256]{1,0:T(8,128)}, f32[256,256]{1,0:T(8,128)}, bf16[256,256]{1,0:T(8,128)(2,1)}) custom-call(bf16[256,256]{1,0:T(8,128)(2,1)} %get-tuple-element.7.out_in, bf16[8,64,256]{2,1,0:T(8,128)(2,1)} %get-tuple-element.8.wall, bf16[256,256]{1,0:T(8,128)(2,1)} %get-tuple-element.9.gfeat_in), custom_call_target="tpu_custom_call" | custom-call | tf_op jit(solution)/shard_map/close/pallas_call | solution.py:541

commit v2 on v1

v2 whole, which is shorter than its diff:
```python
import functools

import jax
import jax.numpy as jnp
from jax import lax
from jax.experimental import pallas as pl
from jax.experimental.pallas import tpu as pltpu
from jax.sharding import PartitionSpec as P

MESH = pl.DeviceIdType.MESH
F32 = jnp.float32
BF16 = jnp.bfloat16
PAIR = 2
PARTS = 4
SPLIT = 2
STRAIGHT = 1
NOW = 0
MAJOR = 1
TAIL = (2, 2)
DIRECT = (1,)
ORDER = 1
KSPLIT = 1
STOP = 99


def remote(src, dst, send, recv, device):
    return pltpu.make_async_remote_copy(
        src_ref=src, dst_ref=dst, send_sem=send, recv_sem=recv, device_id=device, device_id_type=MESH
    )


def cut(width, shares):
    spans, at = [], 0
    for s in shares:
        spans.append((at, width // s))
        at += width // s
    assert at == width
    return spans


def bits_of(n):
    return (n - 1).bit_length()


def xor(a, b, n):
    total = 0
    for k in range(bits_of(n)):
        w = 2**k
        total = total + ((a // w + b // w) % 2) * w
    return total


def mirror(a, n):
    total = 0
    top = bits_of(n)
    for k in range(top):
        total = total + ((a // 2**k) % 2) * 2 ** (top - 1 - k)
    return total


def layer_kernel(
    nrow, nrep, here,
    feat_hbm, wself_hbm, wneigh_hbm, deg_hbm, cot_hbm, tiles_hbm, blocks_hbm, count_hbm,
    out, wall, gfeat,
    wself, wneigh, deg, cot, blocks, count, tiles, runs, adj, keys, tab_v, tab_s, my_feat, src, mine, part, part_in, agg_all, gpre_all,
    dagg, late, acc, late_acc, terms, pair_in, summed, plane_in, back, back_in, straight, straight_in,
    wpart, wrow_in, wrep_in, base, deg_col,
    small_sem, tile_sem, tab_sem, feat_sem, own_sem,
    p1s, p1r, p1ps, p1pr, bs, br, es, er, cs, cr, w1s, w1r, w2s, w2r, w3s, w3r, w3ps, w3pr,
    d0s, d0r, d1s, d1r, d2s, d2r, d3s, d3r, ts, tr, t0s, t0r, t1s, t1r, t2s, t2r,
):
    row, rep = lax.axis_index("row"), lax.axis_index("rep")
    rows, width = feat_hbm.shape
    lanes = src.shape[-1]
    slices = width // lanes
    share = rows // nrep
    half = nrow // PAIR
    tile = tiles.shape[-1]
    slots = tiles.shape[1]
    nblk = rows // tile
    hi, lo = row // PAIR, row % PAIR
    hx, hy = hi % PAIR, hi // PAIR
    ny = half // PAIR
    sx, sy = rep % PAIR, rep // PAIR
    is_src = hi == rep
    is_x = jnp.logical_and(hy == sy, hx != sx)
    is_y = jnp.logical_and(hx == sx, hy != sy)
    is_d = jnp.logical_and(hx != sx, hy != sy)
    partner = (hi * PAIR + (1 - lo), rep)
    my_q = xor(hi, mirror(rep, nrep), nrep)
    owner = (rep * PAIR + lo, my_q)
    moves = jnp.logical_or(owner[0] != row, owner[1] != rep)
    pieces = nrep * SPLIT
    grain = rows // pieces

    def ordered(i):
        place = 0
        for r in range(nrep):
            by_distance = sorted((k for k in range(nrep) if k != r), key=lambda k: (-abs(k - r), k))
            place = place + jnp.where(rep == r, by_distance[i], 0)
        return place

    far = [ordered(i) for i in range(nrep - 1)]

    barrier = pltpu.get_barrier_semaphore()

    def greet(device):
        pl.semaphore_signal(barrier, inc=1, device_id=device, device_id_type=MESH)

    for d in range(1, nrow):
        greet(((row + d) % nrow, rep))
    for d in range(1, nrep):
        greet((row, (rep + d) % nrep))

    for k in range(nrep):
        @pl.when(jnp.logical_or(hi != rep, rep != k))
        def _():
            greet((rep * PAIR + lo, k))
            greet((k * PAIR + lo, hi))

    def own_copy(c, k):
        return pltpu.make_async_copy(
            feat_hbm.at[pl.ds(k * grain, grain), pl.ds(c * lanes, lanes)],
            src.at[c, lo * pieces + k], own_sem.at[c, k],
        )

    @pl.when(is_src)
    def _():
        for c in range(slices):
            for k in range(pieces):
                own_copy(c, k).start()

    small = [
        pltpu.make_async_copy(a, b, small_sem.at[i])
        for i, (a, b) in enumerate((
            (blocks_hbm, blocks), (count_hbm, count), (deg_hbm, deg),
            (wself_hbm, wself), (wneigh_hbm, wneigh), (cot_hbm, cot),
        ))
    ]
    for copy in small:
        copy.start()
    tile_copies = [
        pltpu.make_async_copy(tiles_hbm.at[j], tiles.at[j], tile_sem.at[j]) for j in range(here)
    ]
    for copy in tile_copies:
        copy.start()
    feat_copy = pltpu.make_async_copy(
        feat_hbm.at[pl.ds(pl.multiple_of(rep * share, share), share)], my_feat, feat_sem
    )
    feat_copy.start()

    pl.semaphore_wait(barrier, nrow - 1 + nrep - 1 + 2 * (nrep - is_src.astype(jnp.int32)))

    def hop(c, k, i, h):
        at = src.at[c, lo * pieces + k]
        return remote(at, at, p1s.at[c, k, i], p1r.at[c, k], (h * PAIR + lo, rep))

    def x_peer():
        return hy * PAIR + (1 - hx)

    def y_peer(d):
        return ((hy + d) % ny) * PAIR + hx

    def to_partner(c, k):
        at = src.at[c, lo * pieces + k]
        return remote(at, at, p1ps.at[c, k], p1pr.at[c, k], partner)

    def from_partner(c, k):
        at = src.at[c, (1 - lo) * pieces + k]
        return remote(at, at, p1ps.at[c, k], p1pr.at[c, k], partner)

    first, second = list(range(pieces // 2)), list(range(pieces // 2, pieces))

    @pl.when(is_src)
    def _():
        for c in range(slices):
            for k in range(pieces):
                own_copy(c, k).wait()
            for kx, ky in zip(first + second, second + first):
                hop(c, kx, 0, x_peer()).start()
                for d in range(1, ny):
                    hop(c, ky, d, y_peer(d)).start()
            for k in range(pieces):
                to_partner(c, k).start()

    for copy in small:
        copy.wait()
    side = keys.shape[-1]
    at_row = lax.broadcasted_iota(jnp.int32, (side, side), 0)
    at_col = lax.broadcasted_iota(jnp.int32, (side, side), 1)
    for j in range(here):
        keys[...] = jnp.full(keys.shape, -1, jnp.int32)
        keys[0:1, 0:slots] = blocks[j, 0:1, :] * nblk + blocks[j, 1:2, :]
        line = jnp.broadcast_to(keys[0:1, :], (side, side))
        column = line.T
        before = jnp.where(jnp.logical_and(column == line, at_row < at_col), at_row + 1, 0)
        latest = jnp.where(jnp.logical_and(column == at_col, at_row < count[j]), at_row + 1, 0)
        tab_v[2 * j : 2 * j + 1, :] = jnp.max(before, axis=0, keepdims=True)
        tab_v[2 * j + 1 : 2 * j + 2, :] = jnp.max(latest, axis=0, keepdims=True)
    tab_copy = pltpu.make_async_copy(tab_v, tab_s, tab_sem)
    tab_copy.start()
    run = deg.shape[1]
    for b in range(rows // run):
        line = jnp.broadcast_to(deg[b : b + 1, :].astype(F32), (run, run))
        deg_col[pl.ds(b * run, run), :] = line.T
    tab_copy.wait()

    for j in range(here):
        tile_copies[j].wait()
        runs[0] = jnp.zeros((tile, tile), F32)

        def add(slot, carry):
            runs[slot + 1] = tiles[j, slot].astype(F32) + runs[tab_s[2 * j, slot]]
            return carry

        lax.fori_loop(0, slots, add, 0)

        def place(b, carry):
            for c in range(nblk):
                block = runs[tab_s[2 * j + 1, b * nblk + c]]
                adj[j, pl.ds(pl.multiple_of(b * tile, tile), tile), c * tile : (c + 1) * tile] = block.astype(BF16)
            return carry

        lax.fori_loop(0, nblk, place, 0)

    def relay(c):
        @pl.when(is_x)
        def _():
            for k in first + second:
                hop(c, k, 0, hi).wait_recv()
                if k in first:
                    for d in range(1, ny):
                        hop(c, k, d, y_peer(d)).start()
                to_partner(c, k).start()

        @pl.when(is_y)
        def _():
            for k in second + first:
                hop(c, k, 0, hi).wait_recv()
                if k in second:
                    hop(c, k, 0, x_peer()).start()
                to_partner(c, k).start()

        @pl.when(is_d)
        def _():
            for pair in zip(first, second):
                for k in pair:
                    hop(c, k, 0, hi).wait_recv()
                    to_partner(c, k).start()

        for k in range(pieces):
            from_partner(c, k).wait_recv()

    def partial(c, at, n):
        total = jnp.zeros((n, lanes), F32)
        for j in range(here):
            a = adj[j, pl.ds(pl.multiple_of(at, n), n), :]
            f = src[c, pl.ds(j * pieces, pieces)].reshape(rows, lanes)
            total = total + jnp.dot(a, f, preferred_element_type=F32)
        return total

    last = slices - 1
    step = share // PARTS

    def send_dagg(c, to, i):
        at = dagg.at[c, rep, pl.ds(i * step, step)]
        return remote(at, at, cs.at[c, to, i], cr.at[c, rep, i], (row, to))

    tail = cut(lanes, TAIL)

    def send_late(n, to):
        f0, fs = tail[n]
        at = late.at[rep, pl.ds(f0, fs)]
        return remote(at, at, ts.at[n, to], tr.at[n, rep], (row, to))

    def get_late(n, k):
        f0, fs = tail[n]
        at = late.at[k, pl.ds(f0, fs)]
        return remote(at, at, ts.at[n, k], tr.at[n, k], (row, k))

    def get_dagg(c, k, i):
        at = dagg.at[c, k, pl.ds(i * step, step)]
        return remote(at, at, cs.at[c, k, i], cr.at[c, k, i], (row, k))

    def send_part(c, to):
        return remote(
            part.at[c, to], part_in.at[c, rep], bs.at[c, to], br.at[c, rep], (row, to)
        )

    def get_part(c, k):
        return remote(part_in.at[c, k], part_in.at[c, k], bs.at[c, k], br.at[c, k], (row, k))

    def send_step(to, i):
        steps = pl.ds(i * step, step)
        return remote(
            part.at[last, to, steps], part_in.at[last, rep, steps], es.at[to, i], er.at[rep, i], (row, to)
        )

    def get_step(k, i):
        at = part_in.at[last, k, pl.ds(i * step, step)]
        return remote(at, at, es.at[k, i], er.at[k, i], (row, k))

    def finish(level):
        @pl.when(is_src)
        def _():
            for c in range(slices):
                for k in range(pieces):
                    hop(c, k, 0, x_peer()).wait_send()
                    for d in range(1, ny):
                        hop(c, k, d, y_peer(d)).wait_send()

        @pl.when(is_x)
        def _():
            for c in range(slices):
                for k in first:
                    for d in range(1, ny):
                        hop(c, k, d, y_peer(d)).wait_send()

        @pl.when(is_y)
        def _():
            for c in range(slices):
                for k in second:
                    hop(c, k, 0, x_peer()).wait_send()

        for c in range(slices):
            for k in range(pieces):
                to_partner(c, k).wait_send()
            for to in far:
                if level >= 2:
                    if c < last:
                        send_part(c, to).wait_send()
                    else:
                        for i in range(PARTS):
                            send_step(to, i).wait_send()
                if level >= 3 and c < last:
                    for i in range(PARTS):
                        send_dagg(c, to, i).wait_send()
            if level >= 4 and c < last:
                for q in range(nrep):
                    send_pair(c, q).wait_send()
            if level >= 9 and c < last:
                for e in range(1, half):
                    send_plane(c, e).wait_send()

                @pl.when(moves)
                def _():
                    to_owner(c).wait_send()
        if level >= 3:
            for d in range(1, nrow):
                send_w1(d).wait_send()
        if level >= 9:
            for n in range(len(tail)):
                for q in range(nrep):
                    send_late_pair(n, q).wait_send()
                for to in far:
                    send_late(n, to).wait_send()
                    if n in DIRECT:
                        straight_to(n, to).wait_send()
                if n not in DIRECT:
                    for e in range(1, half):
                        send_late_plane(n, e).wait_send()

                    @pl.when(moves)
                    def _():
                        late_to_owner(n).wait_send()

            @pl.when(jnp.logical_not(is_src))
            def _():
                for n in DIRECT:
                    straight_to(n, rep).wait_send()

        if level >= 9:
            for d in range(1, nrep if not NOW else 1):
                send_w2(d).wait_send()
            for e in range(half if not NOW else 0):
                if e > 0:
                    send_w3(e).wait_send()
                share_w3(e).wait_send()

    for c in range(slices):
        relay(c)
        if STOP == 1:
            continue
        if c < last:
            for to in far:
                part[c, to] = partial(c, to * share, share).astype(BF16)
                send_part(c, to).start()
        elif MAJOR:
            for i in range(PARTS):
                for to in far:
                    part[c, to, pl.ds(i * step, step)] = partial(c, to * share + i * step, step).astype(BF16)
                    send_step(to, i).start()
        else:
            for to in far:
                part[c, to] = partial(c, to * share, share).astype(BF16)
            for i in range(PARTS):
                for to in far:
                    send_step(to, i).start()
        mine[c] = partial(c, rep * share, share)
    feat_copy.wait()
    if STOP == 1:
        finish(1)
        return
    base[...] = jnp.dot(my_feat[...], wself[...], preferred_element_type=F32)

    for c in range(last):
        for k in far:
            get_part(c, k).wait_recv()
            mine[c] = mine[c] + part_in[c, k].astype(F32)
    for i in range(PARTS):
        at = pl.ds(i * step, step)
        degree = deg_col[pl.ds(pl.multiple_of(rep * share + i * step, step), step), :]
        total = mine[last, at]
        for k in far:
            get_step(k, i).wait_recv()
            total = total + part_in[last, k, at].astype(F32)
        sums = [mine[c, at] for c in range(last)] + [total]
        agg = jnp.concatenate([(s / degree).astype(BF16) for s in sums], axis=1)
        agg_all[at] = agg
        pre = base[at] + jnp.dot(agg, wneigh[...], preferred_element_type=F32)
        sig = jax.nn.sigmoid(pre)
        gpre = (cot[at].astype(F32) * sig * (1.0 + pre * (1.0 - sig))).astype(BF16)
        gpre_all[at] = gpre
        back_t = lax.dot_general(gpre, wneigh[...], (((1,), (1,)), ((), ())), preferred_element_type=F32)
        for c in range(slices):
            dagg[c, rep, at] = (back_t[:, c * lanes : (c + 1) * lanes] / degree).astype(BF16)
        if STOP > 2:
            for to in far:
                send_dagg(0, to, i).start()
        out[at] = (pre * sig).astype(BF16)
    if STOP == 2:
        finish(2)
        return
    late[rep] = dagg[last, rep].T
    for n in range(len(tail)):
        for to in far:
            send_late(n, to).start()

    gpre = gpre_all[...]
    ws = lax.dot_general(my_feat[...], gpre, (((0,), (0,)), ((), ())), preferred_element_type=F32)
    wn = lax.dot_general(agg_all[...], gpre, (((0,), (0,)), ((), ())), preferred_element_type=F32)
    piece = wpart.shape[1]
    wpart[pl.ds(0, half)] = ws.astype(BF16).reshape(half, piece, width)
    wpart[pl.ds(half, half)] = wn.astype(BF16).reshape(half, piece, width)

    def send_w1(d):
        to = (row + d) % nrow
        return remote(wpart.at[to], wrow_in.at[d - 1], w1s.at[d - 1], w1r.at[d - 1], (to, rep))

    for d in range(1, nrow):
        send_w1(d).start()
    base[...] = lax.dot_general(gpre, wself[...], (((1,), (1,)), ((), ())), preferred_element_type=F32)

    unit = max(share, 128)
    per_unit = unit // share

    def send_pair(c, q):
        return remote(
            terms.at[c, (1 - lo) * nrep + q], pair_in.at[c, q], d0s.at[c, q], d0r.at[c, q], partner
        )

    def send_plane(c, e):
        return remote(
            summed.at[c, e - 1], plane_in.at[c, e - 1], d1s.at[c, e - 1], d1r.at[c, e - 1],
            (xor(hi, e, half) * PAIR + lo, rep),
        )

    def to_owner(c):
        return remote(back.at[c], back_in.at[c], d2s.at[c], d2r.at[c], owner)

    def straight_to(n, q):
        f0, fs = tail[n]
        return remote(
            straight.at[q, pl.ds(f0, fs)], straight_in.at[hi, pl.ds(f0, fs)],
            d3s.at[n, q], d3r.at[n, hi], (rep * PAIR + lo, q),
        )

    def straight_from(n, k):
        f0, fs = tail[n]
        at = straight_in.at[k, pl.ds(f0, fs)]
        return remote(at, at, d3s.at[n, k], d3r.at[n, k], (k * PAIR + lo, hi))

    def send_late_pair(n, q):
        f0, fs = tail[n]
        return remote(
            terms.at[last, (1 - lo) * nrep + q, pl.ds(f0, fs)], pair_in.at[last, q, pl.ds(f0, fs)],
            t0s.at[n, q], t0r.at[n, q], partner,
        )

    def gain(sums, f0, fs, left, k, start, emit):
        for j in (1 - lo, lo):
            slot = 0 if j is lo else 1
            for u in range(rows // unit):
                a = adj[j, pl.ds(pl.multiple_of(k * share, share), share), u * unit : (u + 1) * unit]
                t = jnp.dot(left, a, preferred_element_type=F32)
                if not start:
                    t = t + sums[slot, u, f0 : f0 + fs, :]
                if emit is None:
                    sums[slot, u, f0 : f0 + fs, :] = t
                    continue
                t = t.astype(BF16)
                for v in range(per_unit):
                    emit(j, u * per_unit + v, t[:, v * share : (v + 1) * share])

    def emit_early(j, q, value):
        terms[0, j * nrep + q] = value
        if j is not lo:
            send_pair(0, q).start()

    def emit_late(n):
        f0, fs = tail[n]

        def emit(j, q, value):
            terms[last, j * nrep + q, f0 : f0 + fs, :] = value
            if j is not lo:
                send_late_pair(n, q).start()

        return emit

    def make_own():
        gain(acc, 0, lanes, dagg[0, rep].T, rep, True, None)
        gain(late_acc, 0, lanes, late[rep], rep, True, None)

    def make_early():
        near = far[::-1]
        for k in near:
            for i in range(PARTS):
                get_dagg(0, k, i).wait_recv()
            gain(acc, 0, lanes, dagg[0, k].T, k, False, emit_early if k is near[-1] else None)

    def make_late(n):
        f0, fs = tail[n]
        near = far[::-1]
        for k in near:
            get_late(n, k).wait_recv()
            gain(late_acc, f0, fs, late[k, f0 : f0 + fs, :], k, False, emit_late(n) if k is near[-1] else None)

    def send_late_plane(n, e):
        f0, fs = tail[n]
        at = (last, e - 1, pl.ds(f0, fs))
        return remote(
            summed.at[at], plane_in.at[at], t1s.at[n, e - 1], t1r.at[n, e - 1],
            (xor(hi, e, half) * PAIR + lo, rep),
        )

    def late_to_owner(n):
        f0, fs = tail[n]
        at = (last, pl.ds(f0, fs))
        return remote(back.at[at], back_in.at[at], t2s.at[n], t2r.at[n], owner)

    def add_late_plane(n):
        f0, fs = tail[n]
        both = back_sum[n + 1]
        for e in range(1, half):
            send_late_plane(n, e).wait_recv()
            both = both + plane_in[last, e - 1, f0 : f0 + fs, :].astype(F32)
        back[last, f0 : f0 + fs, :] = both.astype(BF16)

        @pl.when(moves)
        def _():
            late_to_owner(n).start()

    def add_late_pair(n):
        f0, fs = tail[n]
        if n not in DIRECT:
            for e in list(range(half - 1, 0, -1)) + [0]:
                q = xor(xor(hi, e, half), mirror(rep, nrep), nrep)
                send_late_pair(n, q).wait_recv()
                both = terms[last, lo * nrep + q, f0 : f0 + fs, :].astype(F32)
                both = both + pair_in[last, q, f0 : f0 + fs, :].astype(F32)
                if e > 0:
                    summed[last, e - 1, f0 : f0 + fs, :] = both.astype(BF16)
                    send_late_plane(n, e).start()
                else:
                    back_sum[n + 1] = both
            return
        for q in far + [rep]:
            send_late_pair(n, q).wait_recv()
            both = terms[last, lo * nrep + q, f0 : f0 + fs, :].astype(F32)
            both = (both + pair_in[last, q, f0 : f0 + fs, :].astype(F32)).astype(BF16)
            straight[q, f0 : f0 + fs, :] = both
            if q is rep:
                @pl.when(jnp.logical_not(is_src))
                def _():
                    straight_to(n, q).start()

                @pl.when(is_src)
                def _():
                    straight_in[hi, f0 : f0 + fs, :] = both
            else:
                straight_to(n, q).start()

    def add_pair(c):
        for e in list(range(half - 1, 0, -1)) + [0]:
            q = xor(xor(hi, e, half), mirror(rep, nrep), nrep)
            send_pair(c, q).wait_recv()
            both = terms[c, lo * nrep + q].astype(F32) + pair_in[c, q].astype(F32)
            if e > 0:
                summed[c, e - 1] = both.astype(BF16)
                send_plane(c, e).start()
            else:
                back_sum[c] = both

    def add_plane(c):
        both = back_sum[c]
        for e in range(1, half):
            send_plane(c, e).wait_recv()
            both = both + plane_in[c, e - 1].astype(F32)
        back[c] = both.astype(BF16)

        @pl.when(moves)
        def _():
            to_owner(c).start()

    back_sum = {}
    if NOW:
        for d in range(1, nrow):
            send_w1(d).wait_recv()
    def send_w2(d):
        return remote(
            wrep_in.at[rep], wrep_in.at[rep], w2s.at[d - 1], w2r.at[d - 1], (row, (rep + d) % nrep)
        )

    def send_w3(e):
        return remote(
            wall.at[row], wall.at[row], w3s.at[e - 1], w3r.at[e - 1], (xor(hi, e, half) * PAIR + lo, rep)
        )

    def get_w3(e):
        at = wall.at[xor(hi, e, half) * PAIR + lo]
        return remote(at, at, w3s.at[e - 1], w3r.at[e - 1], (row, rep))

    def share_w3(e):
        at = wall.at[xor(hi, e, half) * PAIR + lo]
        return remote(at, at, w3ps.at[e], w3pr.at[e], partner)

    def shared_w3(e):
        at = wall.at[xor(hi, e, half) * PAIR + (1 - lo)]
        return remote(at, at, w3ps.at[e], w3pr.at[e], partner)

    def reduce_rows():
        wsum = wpart[row].astype(F32)
        for d in range(1, nrow):
            send_w1(d).wait_recv()
            wsum = wsum + wrow_in[d - 1].astype(F32)
        wrep_in[rep] = wsum.astype(BF16)
        for d in range(1, nrep):
            send_w2(d).start()

    def reduce_reps():
        for d in range(1, nrep):
            remote(
                wrep_in.at[rep], wrep_in.at[(rep + nrep - d) % nrep], w2s.at[d - 1], w2r.at[d - 1], (row, rep)
            ).wait_recv()
        wsum = wrep_in[0].astype(F32)
        for k in range(1, nrep):
            wsum = wsum + wrep_in[k].astype(F32)
        wall[row] = wsum.astype(BF16)
        for e in range(1, half):
            send_w3(e).start()
        share_w3(0).start()

    make_own()
    make_early()
    add_pair(0)
    if not NOW:
        reduce_rows()
    for n in range(len(tail)):
        make_late(n)
        add_late_pair(n)
    for c in range(last):
        add_plane(c)
    if ORDER == 1 and not NOW:
        reduce_reps()
    for n in range(len(tail)):
        if n not in DIRECT:
            add_late_plane(n)
    if ORDER == 2 and not NOW:
        reduce_reps()
    if not NOW:
        for e in range(1, half):
            get_w3(e).wait_recv()
            share_w3(e).start()

    for c in range(last):
        cols = slice(c * lanes, (c + 1) * lanes)

        @pl.when(moves)
        def _():
            to_owner(c).wait_recv()
            gfeat[:, cols] = (base[:, cols] + back_in[c].astype(F32).T).astype(BF16)

        @pl.when(jnp.logical_not(moves))
        def _():
            gfeat[:, cols] = (base[:, cols] + back[c].astype(F32).T).astype(BF16)

    for n, (f0, fs) in enumerate(tail):
        if n not in DIRECT:
            cols = slice(last * lanes + f0, last * lanes + f0 + fs)

            @pl.when(moves)
            def _():
                late_to_owner(n).wait_recv()
                gfeat[:, cols] = (base[:, cols] + back_in[last, f0 : f0 + fs, :].astype(F32).T).astype(BF16)

            @pl.when(jnp.logical_not(moves))
            def _():
                gfeat[:, cols] = (base[:, cols] + back[last, f0 : f0 + fs, :].astype(F32).T).astype(BF16)

            continue
        for k in range(half):
            @pl.when(jnp.logical_or(rep != hi, hi != k))
            def _():
                straight_from(n, k).wait_recv()

        both = jnp.zeros((fs, share), F32)
        for k in range(half):
            both = both + straight_in[k, f0 : f0 + fs, :].astype(F32)
        both = both.astype(BF16).astype(F32)
        at = last * lanes + f0
        gfeat[:, at : at + fs] = (base[:, at : at + fs] + both.T).astype(BF16)
    if not NOW:
        for e in range(half):
            shared_w3(e).wait_recv()
    finish(9)


def close_kernel(out_in, wall, gfeat_in, out, gself, gneigh, gfeat):
    half = wall.shape[0] // 2
    out[...] = out_in[...]
    gfeat[...] = gfeat_in[...]
    gself[...] = wall[pl.ds(0, half)].reshape(gself.shape).astype(F32)
    gneigh[...] = wall[pl.ds(half, half)].reshape(gneigh.shape).astype(F32)


def body(
    nrow, nrep,
    features, weight_self, weight_neigh, degrees, tile_values, tile_blocks, tile_count, cotangent,
):
    rows, width = features.shape
    here, slots, tile = tile_values.shape[1], tile_values.shape[2], tile_values.shape[-1]
    share = rows // nrep
    half = nrow // PAIR
    ny = half // PAIR
    piece = 2 * width // nrow
    lanes = 128
    slices = width // lanes
    pieces = nrep * SPLIT
    unit = max(share, 128)
    nt = len(TAIL)
    assert slices == 2 and here == PAIR and half == nrep and (rows // tile) ** 2 <= 128 and slots <= 128
    sems = pltpu.SemaphoreType.DMA
    vmem = pl.BlockSpec(memory_space=pltpu.VMEM)
    anywhere = pl.BlockSpec(memory_space=pl.ANY)

    def buf(*shape):
        return pltpu.VMEM(shape, BF16)

    out, wall, gfeat = pl.pallas_call(
        functools.partial(layer_kernel, nrow, nrep, here),
        out_shape=(
            jax.ShapeDtypeStruct((share, width), BF16),
            jax.ShapeDtypeStruct((nrow, piece, width), BF16),
            jax.ShapeDtypeStruct((share, width), BF16),
        ),
        in_specs=[anywhere] * 8,
        out_specs=(vmem,) * 3,
        scratch_shapes=[
            buf(width, width), buf(width, width),
            pltpu.VMEM((rows // tile, tile), jnp.int32),
            buf(share, width),
            pltpu.VMEM((here, 2, slots), jnp.int32),
            pltpu.SMEM((here,), jnp.int32),
            buf(here, slots, tile, tile),
            pltpu.VMEM((slots + 1, tile, tile), F32),
            buf(here, rows, rows),
            pltpu.VMEM((8, 128), jnp.int32),
            pltpu.VMEM((8, 128), jnp.int32),
            pltpu.SMEM((8, 128), jnp.int32),
            buf(share, width),
            buf(slices, here * pieces, rows // pieces, lanes),
            pltpu.VMEM((slices, share, lanes), F32),
            buf(slices, nrep, share, lanes),
            buf(slices, nrep, share, lanes),
            buf(share, width),
            buf(share, width),
            buf(slices, nrep, share, lanes),
            buf(nrep, lanes, share),
            pltpu.VMEM((here, rows // unit, lanes, unit), F32),
            pltpu.VMEM((here, rows // unit, lanes, unit), F32),
            buf(slices, nrow, lanes, share),
            buf(slices, nrep, lanes, share),
            buf(slices, half - 1, lanes, share),
            buf(slices, half - 1, lanes, share),
            buf(slices, lanes, share),
            buf(slices, lanes, share),
            buf(nrep, lanes, share),
            buf(half, lanes, share),
            buf(nrow, piece, width),
            buf(nrow - 1, piece, width),
            buf(nrep, piece, width),
            pltpu.VMEM((share, width), F32),
            pltpu.VMEM((rows, tile), F32),
            sems((6,)), sems((here,)), sems, sems, sems((slices, pieces)),
            sems((slices, pieces, ny)), sems((slices, pieces)), sems((slices, pieces)), sems((slices, pieces)),
            sems((slices, nrep)), sems((slices, nrep)),
            sems((nrep, PARTS)), sems((nrep, PARTS)),
            sems((slices, nrep, PARTS)), sems((slices, nrep, PARTS)),
            sems((nrow - 1,)), sems((nrow - 1,)),
            sems((nrep - 1,)), sems((nrep - 1,)),
            sems((half - 1,)), sems((half - 1,)), sems((half,)), sems((half,)),
            sems((slices, nrep)), sems((slices, nrep)),
            sems((slices, half - 1)), sems((slices, half - 1)),
            sems((slices,)), sems((slices,)),
            sems((nt, nrep)), sems((nt, half)), sems((nt, nrep)), sems((nt, nrep)),
            sems((nt, nrep)), sems((nt, nrep)),
            sems((nt, half - 1)), sems((nt, half - 1)), sems((nt,)), sems((nt,)),
        ],
        compiler_params=pltpu.CompilerParams(collective_id=0, has_side_effects=True),
        name="layer",
    )(
        features, weight_self, weight_neigh, degrees.reshape(rows // tile, tile), cotangent,
        tile_values[0], tile_blocks.transpose(0, 1, 3, 2)[0], tile_count[0],
    )
    out, grad_self, grad_neigh, gfeat = pl.pallas_call(
        close_kernel,
        out_shape=(
            jax.ShapeDtypeStruct((share, width), BF16),
            jax.ShapeDtypeStruct((width, width), F32),
            jax.ShapeDtypeStruct((width, width), F32),
            jax.ShapeDtypeStruct((share, width), BF16),
        ),
        in_specs=[vmem] * 3,
        out_specs=(vmem,) * 4,
        name="close",
    )(out, wall, gfeat)
    return out, grad_self, grad_neigh, gfeat


def solution(mesh):
    in_specs = (
        P("row", None),
        P(),
        P(),
        P("row"),
        P("row", "rep", None, None, None),
        P("row", "rep", None, None),
        P("row", "rep"),
        P(("row", "rep"), None),
    )
    out_specs = (P(("row", "rep"), None), P(), P(), P(("row", "rep"), None))
    run = functools.partial(body, mesh.shape["row"], mesh.shape["rep"])
    return jax.shard_map(run, mesh=mesh, in_specs=in_specs, out_specs=out_specs, check_vma=False)
```

time: 58.7 us -> 56.2 us (0.957)
  the two profiles are of different devices: /device:TPU:0 before, /device:TPU:13 now
where the time goes in v2:
time: 56.2 us; the launch traced here: 56.1 us
  Pallas kernels  55.4 us (99%)
  between operations  0.64 us (1%)
    pallas_call x1, Pallas kernels, body(): pl.pallas_call(functools.partial(layer_kernel, nrow, nrep, here), out_sha...  53.5 us
    pallas_call x1, Pallas kernels, body(): pl.pallas_call(close_kernel, out_shape=(jax.ShapeDtypeStruct((share, widt...  1.95 us

profile of v2, /device:TPU:13, one launch (start us, length us, event | category | flops | bytes accessed | tf_op | source)
XLA Modules:
  0.0 56.1 jit_solution(10575428313170029329)
XLA Ops:
  0.6 53.5 %layer.1 = (bf16[256,256]{1,0:T(8,128)(2,1)}, bf16[8,64,256]{2,1,0:T(8,128)(2,1)}, bf16[256,256]{1,0:T(8,128)(2,1)}) custom-call(bf16[1024,256]{1,0:T(8,128)(2,1)} %feat_hbm.1, bf16[256,256]{1,0:T(8,128)(2,1)} %wself_hbm.1, bf16[256,256]{1,0:T(8,128)(2,1)} %wneigh_hbm.1, s32[8,128]{1,0:T(8,128)} %bitcast.7, bf16[256,256]{1,0:T(8,128)(2,1)} %cot_hbm.1, ...), custom_call_target="tpu_custom_call" | custom-call | tf_op jit(solution)/shard_map/layer/pallas_call | solution.py:759
  54.1 1.9 %close.1 = (bf16[256,256]{1,0:T(8,128)(2,1)}, f32[256,256]{1,0:T(8,128)}, f32[256,256]{1,0:T(8,128)}, bf16[256,256]{1,0:T(8,128)(2,1)}) custom-call(bf16[256,256]{1,0:T(8,128)(2,1)} %get-tuple-element.7.out_in, bf16[8,64,256]{2,1,0:T(8,128)(2,1)} %get-tuple-element.8.wall, bf16[256,256]{1,0:T(8,128)(2,1)} %get-tuple-element.9.gfeat_in), custom_call_target="tpu_custom_call" | custom-call | tf_op jit(solution)/shard_map/close/pallas_call | solution.py:825

commit v3 on v2

--- a/solution.py
+++ b/solution.py
@@ -13,14 +13,8 @@
 PAIR = 2
 PARTS = 4
 SPLIT = 2
-STRAIGHT = 1
-NOW = 0
-MAJOR = 1
-TAIL = (2, 2)
+TAIL = (5, 3)
 DIRECT = (1,)
-ORDER = 1
-KSPLIT = 1
-STOP = 99
 
 
 def remote(src, dst, send, recv, device):
@@ -32,8 +26,8 @@
 def cut(width, shares):
     spans, at = [], 0
     for s in shares:
-        spans.append((at, width // s))
-        at += width // s
+        spans.append((at, width * s // sum(shares)))
+        at += width * s // sum(shares)
     assert at == width
     return spans
 
@@ -300,7 +294,7 @@
         at = part_in.at[last, k, pl.ds(i * step, step)]
         return remote(at, at, es.at[k, i], er.at[k, i], (row, k))
 
-    def finish(level):
+    def finish_sums():
         @pl.when(is_src)
         def _():
             for c in range(slices):
@@ -325,82 +319,69 @@
         for c in range(slices):
             for k in range(pieces):
                 to_partner(c, k).wait_send()
-            for to in far:
-                if level >= 2:
-                    if c < last:
-                        send_part(c, to).wait_send()
-                    else:
-                        for i in range(PARTS):
-                            send_step(to, i).wait_send()
-                if level >= 3 and c < last:
-                    for i in range(PARTS):
-                        send_dagg(c, to, i).wait_send()
-            if level >= 4 and c < last:
-                for q in range(nrep):
-                    send_pair(c, q).wait_send()
-            if level >= 9 and c < last:
+        for to in far:
+            for c in range(last):
+                send_part(c, to).wait_send()
+            for i in range(PARTS):
+                send_step(to, i).wait_send()
+
+    def finish_gather():
+        for to in far:
+            for i in range(PARTS):
+                send_dagg(0, to, i).wait_send()
+            for n in range(len(tail)):
+                send_late(n, to).wait_send()
+        for d in range(1, nrow):
+            send_w1(d).wait_send()
+        for q in range(nrep):
+            send_pair(0, q).wait_send()
+
+    def finish_rest():
+        for e in range(1, half):
+            send_plane(0, e).wait_send()
+
+        @pl.when(moves)
+        def _():
+            to_owner(0).wait_send()
+
+        for n in range(len(tail)):
+            for q in range(nrep):
+                send_late_pair(n, q).wait_send()
+            if n in DIRECT:
+                for to in far:
+                    straight_to(n, to).wait_send()
+
+                @pl.when(jnp.logical_not(is_src))
+                def _():
+                    straight_to(n, rep).wait_send()
+            else:
                 for e in range(1, half):
-                    send_plane(c, e).wait_send()
+                    send_late_plane(n, e).wait_send()
 
                 @pl.when(moves)
                 def _():
-                    to_owner(c).wait_send()
-        if level >= 3:
-            for d in range(1, nrow):
-                send_w1(d).wait_send()
-        if level >= 9:
-            for n in range(len(tail)):
-                for q in range(nrep):
-                    send_late_pair(n, q).wait_send()
-                for to in far:
-                    send_late(n, to).wait_send()
-                    if n in DIRECT:
-                        straight_to(n, to).wait_send()
-                if n not in DIRECT:
-                    for e in range(1, half):
-                        send_late_plane(n, e).wait_send()
-
-                    @pl.when(moves)
-                    def _():
-                        late_to_owner(n).wait_send()
-
-            @pl.when(jnp.logical_not(is_src))
-            def _():
-                for n in DIRECT:
-                    straight_to(n, rep).wait_send()
-
-        if level >= 9:
-            for d in range(1, nrep if not NOW else 1):
-                send_w2(d).wait_send()
-            for e in range(half if not NOW else 0):
-                if e > 0:
-                    send_w3(e).wait_send()
-                share_w3(e).wait_send()
+                    late_to_owner(n).wait_send()
+
+        for d in range(1, nrep):
+            send_w2(d).wait_send()
+        for e in range(half):
+            if e > 0:
+                send_w3(e).wait_send()
+            share_w3(e).wait_send()
 
     for c in range(slices):
         relay(c)
-        if STOP == 1:
-            continue
         if c < last:
             for to in far:
                 part[c, to] = partial(c, to * share, share).astype(BF16)
                 send_part(c, to).start()
-        elif MAJOR:
+        else:
             for i in range(PARTS):
                 for to in far:
                     part[c, to, pl.ds(i * step, step)] = partial(c, to * share + i * step, step).astype(BF16)
                     send_step(to, i).start()
-        else:
-            for to in far:
-                part[c, to] = partial(c, to * share, share).astype(BF16)
-            for i in range(PARTS):
-                for to in far:
-                    send_step(to, i).start()
         mine[c] = partial(c, rep * share, share)
     feat_copy.wait()
-    if STOP == 1:
-        finish(1)
-        return
     base[...] = jnp.dot(my_feat[...], wself[...], preferred_element_type=F32)
 
     for c in range(last):
@@ -424,13 +405,9 @@
         back_t = lax.dot_general(gpre, wneigh[...], (((1,), (1,)), ((), ())), preferred_element_type=F32)
         for c in range(slices):
             dagg[c, rep, at] = (back_t[:, c * lanes : (c + 1) * lanes] / degree).astype(BF16)
-        if STOP > 2:
-            for to in far:
-                send_dagg(0, to, i).start()
+        for to in far:
+            send_dagg(0, to, i).start()
         out[at] = (pre * sig).astype(BF16)
-    if STOP == 2:
-        finish(2)
-        return
     late[rep] = dagg[last, rep].T
     for n in range(len(tail)):
         for to in far:
@@ -613,9 +590,6 @@
             to_owner(c).start()
 
     back_sum = {}
-    if NOW:
-        for d in range(1, nrow):
-            send_w1(d).wait_recv()
     def send_w2(d):
         return remote(
             wrep_in.at[rep], wrep_in.at[rep], w2s.at[d - 1], w2r.at[d - 1], (row, (rep + d) % nrep)
@@ -661,26 +635,23 @@
         share_w3(0).start()
 
     make_own()
+    finish_sums()
     make_early()
     add_pair(0)
-    if not NOW:
-        reduce_rows()
+    reduce_rows()
     for n in range(len(tail)):
         make_late(n)
         add_late_pair(n)
+    finish_gather()
     for c in range(last):
         add_plane(c)
-    if ORDER == 1 and not NOW:
-        reduce_reps()
+    reduce_reps()
     for n in range(len(tail)):
         if n not in DIRECT:
             add_late_plane(n)
-    if ORDER == 2 and not NOW:
-        reduce_reps()
-    if not NOW:
-        for e in range(1, half):
-            get_w3(e).wait_recv()
-            share_w3(e).start()
+    for e in range(1, half):
+        get_w3(e).wait_recv()
+        share_w3(e).start()
 
     for c in range(last):
         cols = slice(c * lanes, (c + 1) * lanes)
@@ -719,10 +690,9 @@
         both = both.astype(BF16).astype(F32)
         at = last * lanes + f0
         gfeat[:, at : at + fs] = (base[:, at : at + fs] + both.T).astype(BF16)
-    if not NOW:
-        for e in range(half):
-            shared_w3(e).wait_recv()
-    finish(9)
+    for e in range(half):
+        shared_w3(e).wait_recv()
+    finish_rest()
 
 
 def close_kernel(out_in, wall, gfeat_in, out, gself, gneigh, gfeat):
@@ -751,7 +721,7 @@
     assert slices == 2 and here == PAIR and half == nrep and (rows // tile) ** 2 <= 128 and slots <= 128
     sems = pltpu.SemaphoreType.DMA
     vmem = pl.BlockSpec(memory_space=pltpu.VMEM)
-    anywhere = pl.BlockSpec(memory_space=pl.ANY)
+    anywhere = pl.BlockSpec(memory_space=pltpu.HBM)
 
     def buf(*shape):
         return pltpu.VMEM(shape, BF16)
@@ -816,12 +786,17 @@
             sems((nt, nrep)), sems((nt, nrep)),
             sems((nt, half - 1)), sems((nt, half - 1)), sems((nt,)), sems((nt,)),
         ],
-        compiler_params=pltpu.CompilerParams(collective_id=0, has_side_effects=True),
+        compiler_params=pltpu.CompilerParams(
+            collective_id=0, has_side_effects=True, vmem_limit_bytes=44 * 2**20
+        ),
         name="layer",
-    )(
-        features, weight_self, weight_neigh, degrees.reshape(rows // tile, tile), cotangent,
-        tile_values[0], tile_blocks.transpose(0, 1, 3, 2)[0], tile_count[0],
-    )
+    )(*(
+        pltpu.with_memory_space_constraint(x, pltpu.HBM)
+        for x in (
+            features, weight_self, weight_neigh, degrees.reshape(rows // tile, tile), cotangent,
+            tile_values[0], tile_blocks.transpose(0, 1, 3, 2)[0], tile_count[0],
+        )
+    ))
     out, grad_self, grad_neigh, gfeat = pl.pallas_call(
         close_kernel,
         out_shape=(
@@ -832,6 +807,7 @@
         ),
         in_specs=[vmem] * 3,
         out_specs=(vmem,) * 4,
+        compiler_params=pltpu.CompilerParams(vmem_limit_bytes=8 * 2**20),
         name="close",
     )(out, wall, gfeat)
     return out, grad_self, grad_neigh, gfeat

time: 56.2 us -> 54.2 us (0.964)
  Pallas kernels: 55.4 us -> 53.4 us
    pallas_call x1, Pallas kernels: 53.5 us -> 52.4 us  [body(): pl.pallas_call(functools.partial(layer_kernel, nrow, nrep, here), out_sha...]
    pallas_call x1, Pallas kernels: 1.95 us -> 0.92 us  [body(): pl.pallas_call(close_kernel, out_shape=(jax.ShapeDtypeStruct((share, widt...]
where the time goes in v3:
time: 54.2 us; the launch traced here: 54 us
  Pallas kernels  53.4 us (99%)
  between operations  0.64 us (1%)
    pallas_call x1, Pallas kernels, body(): pl.pallas_call(functools.partial(layer_kernel, nrow, nrep, here), out_sha...  52.4 us

profile of v3, /device:TPU:13, one launch (start us, length us, event | category | flops | bytes accessed | tf_op | source)
XLA Modules:
  0.0 54.0 jit_solution(7146420114676918848)
XLA Ops:
  0.6 52.4 %layer.1 = (bf16[256,256]{1,0:T(8,128)(2,1)S(1)}, bf16[8,64,256]{2,1,0:T(8,128)(2,1)S(1)}, bf16[256,256]{1,0:T(8,128)(2,1)S(1)}) custom-call(bf16[1024,256]{1,0:T(8,128)(2,1)} %feat_hbm.1, bf16[256,256]{1,0:T(8,128)(2,1)} %wself_hbm.1, bf16[256,256]{1,0:T(8,128)(2,1)} %wneigh_hbm.1, s32[8,128]{1,0:T(8,128)} %bitcast.7, bf16[256,256]{1,0:T(8,128)(2,1)} %cot_hbm.1, ...), custom_call_target="tpu_custom_call" | custom-call | tf_op jit(solution)/shard_map/layer/pallas_call | solution.py:729
  53.1 0.9 %close.1 = (bf16[256,256]{1,0:T(8,128)(2,1)}, f32[256,256]{1,0:T(8,128)}, f32[256,256]{1,0:T(8,128)}, bf16[256,256]{1,0:T(8,128)(2,1)}) custom-call(bf16[256,256]{1,0:T(8,128)(2,1)S(1)} %get-tuple-element.7.out_in, bf16[8,64,256]{2,1,0:T(8,128)(2,1)S(1)} %get-tuple-element.8.wall, bf16[256,256]{1,0:T(8,128)(2,1)S(1)} %get-tuple-element.9.gfeat_in), custom_call_target="tpu_custom_call" | custom-call | tf_op jit(solution)/shard_map/close/pallas_call | solution.py:800

commit v4 on v3

--- a/solution.py
+++ b/solution.py
@@ -12,7 +12,7 @@
 BF16 = jnp.bfloat16
 PAIR = 2
 PARTS = 4
-SPLIT = 2
+SPLIT = 1
 TAIL = (5, 3)
 DIRECT = (1,)
 
@@ -637,8 +637,8 @@
     make_own()
     finish_sums()
     make_early()
+    reduce_rows()
     add_pair(0)
-    reduce_rows()
     for n in range(len(tail)):
         make_late(n)
         add_late_pair(n)

time: 54.2 us -> 53.7 us (level)
  no operation moved by 1% of the time
where the time goes in v4:
time: 53.7 us; the launch traced here: 53.6 us
  Pallas kernels  52.9 us (99%)
  between operations  0.64 us (1%)
    pallas_call x1, Pallas kernels, body(): pl.pallas_call(functools.partial(layer_kernel, nrow, nrep, here), out_sha...  52 us

profile of v4, /device:TPU:13, one launch (start us, length us, event | category | flops | bytes accessed | tf_op | source)
XLA Modules:
  0.0 53.6 jit_solution(16701477417432971919)
XLA Ops:
  0.6 52.0 %layer.1 = (bf16[256,256]{1,0:T(8,128)(2,1)S(1)}, bf16[8,64,256]{2,1,0:T(8,128)(2,1)S(1)}, bf16[256,256]{1,0:T(8,128)(2,1)S(1)}) custom-call(bf16[1024,256]{1,0:T(8,128)(2,1)} %feat_hbm.1, bf16[256,256]{1,0:T(8,128)(2,1)} %wself_hbm.1, bf16[256,256]{1,0:T(8,128)(2,1)} %wneigh_hbm.1, s32[8,128]{1,0:T(8,128)} %bitcast.7, bf16[256,256]{1,0:T(8,128)(2,1)} %cot_hbm.1, ...), custom_call_target="tpu_custom_call" | custom-call | tf_op jit(solution)/shard_map/layer/pallas_call | solution.py:729
  52.7 0.9 %close.1 = (bf16[256,256]{1,0:T(8,128)(2,1)}, f32[256,256]{1,0:T(8,128)}, f32[256,256]{1,0:T(8,128)}, bf16[256,256]{1,0:T(8,128)(2,1)}) custom-call(bf16[256,256]{1,0:T(8,128)(2,1)S(1)} %get-tuple-element.7.out_in, bf16[8,64,256]{2,1,0:T(8,128)(2,1)S(1)} %get-tuple-element.8.wall, bf16[256,256]{1,0:T(8,128)(2,1)S(1)} %get-tuple-element.9.gfeat_in), custom_call_target="tpu_custom_call" | custom-call | tf_op jit(solution)/shard_map/close/pallas_call | solution.py:800
